TPU v7x, 128 devices: a whole 4x4x4 slice. The times are simulated.
128 devices in a mesh: ctx: 8 (over y, x_hi), head: 16 (over x_lo, z, core).
Axes of the slice: x: 4 (x_hi: 2, x_lo: 2; x = x_hi * 2 + x_lo), y: 4, z: 4, core: 2. Of those that a mesh axis runs over, the one named last changes fastest.
Arguments:
- queries: bfloat16 [2, 4096, 4096], P(None, 'ctx', 'head'), may hold values from -6 to 6
- keys: bfloat16 [2, 4096, 4096], P(None, 'ctx', 'head'), may hold values from -6 to 6
- values: bfloat16 [2, 4096, 4096], P(None, 'ctx', 'head'), may hold values from -6 to 6
- rates: float32 [16, 2, 4096], P('head', None, 'ctx'), may hold values from 0.05 to 1
- w_gate: float32 [16, 256, 512], P('head'), may hold values from -0.375 to 0.375
- w_up: float32 [16, 256, 512], P('head'), may hold values from -0.375 to 0.375
- w_down: float32 [16, 512, 256], P('head'), may hold values from -0.25 to 0.25
- gains: float32 [16, 256], P('head'), may hold values from 0.25 to 0.6
- out_proj: bfloat16 [4096, 4096], P('head'), may hold values from -0.125 to 0.125
Outputs:
- output: bfloat16 [2, 4096, 4096], P(None, 'ctx', 'head')
All inputs are finite; a program needn't handle non-finite values.
Results may differ from a plain program's by a relative error of at most 0.0051.
Values may be sent and summed in bfloat16 or wider, within the bound.
A program may use at most 128 MiB of HBM per device.

v0:
```python
import jax
import jax.numpy as jnp
from jax import lax
from jax.sharding import PartitionSpec as P

WINDOW = 256
NS_ITERS = 5
highest = lax.Precision.HIGHEST
attn_temp = 5.0
step_size = 0.5
quintic_one = 3.4445
quintic_two = -4.775
quintic_three = 2.0315


def passed_along(value, axis, steps):
    count = lax.axis_size(axis)
    pairs = [(source, (source + steps) % count) for source in range(count)]
    return lax.ppermute(value, axis, pairs)


def unit_rows(matrix):
    return matrix / jnp.sqrt(jnp.sum(matrix * matrix, axis=-1, keepdims=True) + 1e-06)


def exact_dot(left, right):
    return jnp.dot(left, right, precision=highest, preferred_element_type=jnp.float32)


def fast_grads(key_unit, value_rows, rate_rows, w_gate, w_up, w_down):
    gate_pre = exact_dot(key_unit, w_gate)
    up_pre = exact_dot(key_unit, w_up)
    sigma = jax.nn.sigmoid(gate_pre)
    gate_act = gate_pre * sigma
    hidden = gate_act * up_pre
    target = rate_rows[:, None] * value_rows
    grad_down = exact_dot(hidden.T, target)
    back_hidden = exact_dot(target, w_down.T)
    slope = sigma * (1.0 + gate_pre * (1.0 - sigma))
    grad_gate = exact_dot(key_unit.T, back_hidden * up_pre * slope)
    grad_up = exact_dot(key_unit.T, back_hidden * gate_act)
    return jnp.stack([grad_gate, grad_up, grad_down.T])


def quintic_step(gram, iterate):
    poly = quintic_two * gram + quintic_three * jnp.einsum(
        "mij,mjk->mik", gram, gram, precision=highest
    )
    return quintic_one * iterate + jnp.einsum("mij,mjk->mik", poly, iterate, precision=highest)


def orthogonal(grads):
    norms = jnp.sqrt(jnp.sum(grads * grads, axis=(1, 2), keepdims=True)) + 1e-06
    iterate = grads / norms
    for sweep_at in range(NS_ITERS):
        gram = jnp.einsum("mik,mjk->mij", iterate, iterate, precision=highest)
        iterate = quintic_step(gram, iterate)
    return iterate


def apply_fast(query_unit, w_gate, w_up, w_down):
    gate_pre = exact_dot(query_unit, w_gate)
    gate_act = gate_pre * jax.nn.sigmoid(gate_pre)
    return exact_dot(gate_act * exact_dot(query_unit, w_up), w_down)


def band_attention(query_half, ext_keys, ext_values, masked_head):
    local_rows = query_half.shape[0]
    block_rows = min(512, local_rows)
    scores = lax.dot_general(
        query_half, ext_keys, (((1,), (1,)), ((), ())), preferred_element_type=jnp.float32
    )
    query_pos = jnp.arange(block_rows, dtype=jnp.int32)[:, None]
    key_pos = jnp.arange(block_rows + WINDOW, dtype=jnp.int32)[None, :]
    distance = query_pos + WINDOW - key_pos
    valid = (distance >= 0) & (distance < WINDOW)
    if masked_head is not None:
        valid = valid & ((key_pos + 0 >= WINDOW) | jnp.logical_not(masked_head))
    weights = jnp.where(valid, jnp.exp(attn_temp * (scores - 1.0)), 0.0)
    probs = (weights / jnp.sum(weights, axis=-1, keepdims=True)).astype(jnp.bfloat16)
    outputs = jnp.dot(probs, ext_values, preferred_element_type=jnp.float32)
    return outputs


def body(queries, keys, values, rates, w_gate, w_up, w_down, gains, out_proj):
    group_count, local_rows, head_width = queries.shape
    first_device = lax.axis_index("ctx") == 0
    query_unit = unit_rows(queries.astype(jnp.float32))
    key_unit = unit_rows(keys.astype(jnp.float32))
    query_half = query_unit.astype(jnp.bfloat16)
    key_half = key_unit.astype(jnp.bfloat16)
    tails = jnp.stack([key_half[:, local_rows - WINDOW :], values[:, local_rows - WINDOW :]])
    prior = passed_along(tails, "ctx", 1)
    gate_now = w_gate[0]
    up_now = w_up[0]
    down_now = w_down[0]
    mixed = []
    for group_at in range(group_count):
        if group_at == 0:
            halo_rows = prior[:, 0]
            masked_head = first_device
        else:
            halo_rows = jnp.where(first_device, prior[:, group_at - 1], prior[:, group_at])
            masked_head = None
        ext_keys = jnp.concatenate([halo_rows[0], key_half[group_at]], axis=0)
        ext_values = jnp.concatenate([halo_rows[1], values[group_at]], axis=0)
        attended = band_attention(query_half[group_at], ext_keys, ext_values, masked_head)
        grads = fast_grads(
            key_unit[group_at],
            values[group_at].astype(jnp.float32),
            rates[0, group_at],
            gate_now,
            up_now,
            down_now,
        )
        ortho = orthogonal(lax.psum(grads, "ctx"))
        gate_now = gate_now + step_size * ortho[0]
        up_now = up_now + step_size * ortho[1]
        down_now = down_now + step_size * ortho[2].T
        fast_out = apply_fast(query_unit[group_at], gate_now, up_now, down_now)
        normed = (
            fast_out
            * lax.rsqrt(jnp.mean(fast_out * fast_out, axis=-1, keepdims=True) + 1e-05)
            * gains[0]
        )
        mixed.append((attended + normed).astype(jnp.bfloat16))
    combined = jnp.stack(mixed)
    proj_columns = lax.all_to_all(out_proj, "head", split_axis=1, concat_axis=0, tiled=True)
    summed = jnp.einsum(
        "ctf,fo->cto",
        lax.all_gather(combined, "head", axis=2, tiled=True),
        proj_columns,
        preferred_element_type=jnp.float32,
    )
    return summed.astype(jnp.bfloat16)


def solution(mesh):
    return jax.shard_map(
        body,
        mesh=mesh,
        in_specs=(
            P(None, "ctx", "head"),
            P(None, "ctx", "head"),
            P(None, "ctx", "head"),
            P("head", None, "ctx"),
            P("head", None, None),
            P("head", None, None),
            P("head", None, None),
            P("head", None),
            P("head", None),
        ),
        out_specs=P(None, "ctx", "head"),
        check_vma=False,
    )
```

profile of v0, /device:TPU:1, one launch (start us, length us, event | category | flops | bytes accessed | tf_op | source)
XLA Modules:
  0.0 370.9 jit_solution(8970687296122975035)
XLA Ops:
  6.5 1.3 fusion.18
  7.9 1.2 convert_divide_fusion
  10.1 3.6 collective-permute-start
  13.6 1.0 fusion.61
  14.7 1.0 fusion.63
  15.7 1.1 fusion.52
  16.8 1.3 convolution_bitcast_fusion.4
  18.1 1.4 convolution_bitcast_fusion.5
  19.5 1.4 convolution_bitcast_fusion.3
  20.9 1.3 pad_maximum_fusion
  23.4 1.3 fusion.17
  24.8 1.0 copy.10
  26.6 1.2 convert_divide_fusion.1
  28.0 1.1 slice_select_fusion
  29.7 1.6 slice_bitcast_fusion.28
  31.4 2.0 fusion.127
  33.4 82.0 %all-reduce.3.cloned.1.call-done = f32[3,256,512]{2,1,0:T(8,128)} async-done(((f32[3,256,512]{2,1,0:T(8,128)}), f32[3,256,512]{2,1,0:T(8,128)}) %all-reduce.3.cloned.1.call-update) | async-done | bytes 1572880 | tf_op jit(solution)/shard_map/psum | solution.py:116
  115.4 1.8 multiply_reduce_fusion.1
  117.3 1.8 fusion.85
  119.1 0.9 fusion.12
  120.1 1.8 multiply_add_fusion.9
  121.9 1.7 fusion.128
  124.5 1.6 multiply_add_fusion.8
  126.1 1.8 fusion.129
  128.9 1.6 multiply_add_fusion.7
  130.4 1.7 fusion.130
  132.1 0.9 fusion.9
  133.0 1.6 multiply_add_fusion.6
  134.6 1.7 fusion.131
  137.2 1.6 multiply_add_fusion.5
  138.8 1.0 fusion.57
  139.9 1.5 fusion.54
  141.4 1.1 fusion.66
  142.5 1.3 convolution_bitcast_fusion.1
  143.8 1.4 convolution_bitcast_fusion.2
  145.2 1.4 convolution_bitcast_fusion
  146.6 1.3 pad_maximum_fusion.1
  147.9 1.0 copy-done.17
  149.0 2.0 fusion.126
  150.9 1.0 fusion.59
  152.0 1.2 convolution_multiply_fusion.1
  153.2 1.9 multiply_reduce_fusion.3
  155.1 2.0 copy.11
  157.1 2.8 fusion.16
  159.9 83.1 %all-reduce.5.cloned.1.call-done = f32[3,256,512]{2,1,0:T(8,128)} async-done(((f32[3,256,512]{2,1,0:T(8,128)}), f32[3,256,512]{2,1,0:T(8,128)}) %all-reduce.5.cloned.1.call-update) | async-done | bytes 1572880 | tf_op jit(solution)/shard_map/psum | solution.py:116
  243.0 1.8 multiply_reduce_fusion
  244.9 1.8 fusion.86
  246.7 0.9 fusion.7
  247.6 1.8 multiply_add_fusion.4
  249.4 1.7 fusion.132
  252.1 1.8 multiply_add_fusion.3
  253.8 1.7 fusion.133
  256.4 1.6 multiply_add_fusion.2
  258.0 1.7 fusion.134
  260.6 1.6 multiply_add_fusion.1
  262.2 1.7 fusion.135
  264.8 1.8 multiply_add_fusion
  266.6 1.1 fusion.46
  267.7 1.2 convolution_multiply_fusion
  268.9 1.2 multiply_reduce_fusion.2
  270.3 2.0 fusion.15
  273.4 43.4 %all_to_all.19 = bf16[256,16,256]{2,0,1:T(8,128)(2,1)S(1)} all-to-all(bf16[256,16,256]{2,0,1:T(8,128)(2,1)S(1)} %bitcast.208), channel_id=1, replica_groups=mesh['ctx'=8,'head'=16] {'head'}, dimensions={1} | all-to-all | bytes 4194304 | tf_op jit(solution)/shard_map/all_to_all | solution.py:128
  316.9 40.8 %all-gather.2.cloned.1.call-done = bf16[2,512,4096]{2,1,0:T(8,128)(2,1)} async-done(((bf16[2,512,256]{2,1,0:T(8,128)(2,1)}), bf16[2,512,4096]{2,1,0:T(8,128)(2,1)}) %all-gather.2.cloned.1.call-update) | async-done | bytes 8388624 | tf_op jit(solution)/shard_map/all_gather | solution.py:131
  357.6 6.5 %convolution_convert_fusion = bf16[2,512,256]{2,1,0:T(8,128)(2,1)} fusion(bf16[2,512,4096]{2,1,0:T(8,128)(2,1)} %all-gather.2.cloned.1.call-done, bf16[4096,256,1]{1,0,2:T(8,128)(2,1)S(1)} %bitcast.210), kind=kOutput, calls=%fused_computation.29 | convolution fusion | flops 2147745792 | bytes 11010048 | tf_op jit(solution)/shard_map/ctf,fo->cto/dot_general | solution.py:129
  (76 shorter events, 12.1 us)
Async XLA Ops:
  6.5 2.6 copy-start.5
  6.5 108.9 %all-reduce.3.cloned.1.call-start = ((), (), s32[]{:S(2)}) async-start(), calls=%async_computation.1 | async-start | bytes 3145728 | tf_op jit(solution)/shard_map/psum | solution.py:116
  9.1 4.5 %copy-start.21 = (f32[1,2,512]{2,1,0:T(2,128)S(1)}, f32[1,2,512]{2,1,0:T(2,128)}, u32[]{:S(2)}) copy-start(f32[1,2,512]{2,1,0:T(2,128)} %param.12) | copy-start | bytes 12292
  9.1 4.5 %copy-start = (f32[1,256,512]{2,1,0:T(8,128)S(1)}, f32[1,256,512]{2,1,0:T(8,128)}, u32[]{:S(2)}) copy-start(f32[1,256,512]{2,1,0:T(8,128)} %param.13) | copy-start | bytes 1572868
  9.2 5.5 %copy-start.8 = (f32[1,256,512]{2,1,0:T(8,128)S(1)}, f32[1,256,512]{2,1,0:T(8,128)}, u32[]{:S(2)}) copy-start(f32[1,256,512]{2,1,0:T(8,128)} %param.14) | copy-start | bytes 1572868
  10.1 17.9 %collective-permute-start = (bf16[2,2,256,256]{3,2,1,0:T(8,128)(2,1)}, bf16[2,2,256,256]{3,2,1,0:T(8,128)(2,1)}, u32[]{:S(2)}, u32[]{:S(2)}) collective-permute-start(bf16[2,2,256,256]{3,2,1,0:T(8,128)(2,1)} %pad_maximum_fusion.2), channel_id=1, source_target_pairs={{0,16},{16,32},{32,48},{48,64},{64,80},{80,96},{96,112},{112,0},{1... | collective-permute-start | bytes 1572872 | tf_op jit(solution)/shard_map/ppermute | solution.py:19
  14.7 1.0 copy-start.11
  22.1 2.7 copy-start.12
  22.2 220.8 %all-reduce.5.cloned.1.call-start = ((), (), s32[]{:S(2)}) async-start(), calls=%async_computation.2 | async-start | bytes 3145728 | tf_op jit(solution)/shard_map/psum | solution.py:116
  23.4 3.1 copy-start.13
  27.8 5.6 %copy-start.16 = (bf16[2,512,256]{2,1,0:T(8,128)(2,1)}, bf16[2,512,256]{2,1,0:T(8,128)(2,1)S(1)}, u32[]{:S(2)}) copy-start(bf16[2,512,256]{2,1,0:T(8,128)(2,1)S(1)} %get-tuple-element.6) | copy-start | bytes 1572868
  115.4 1.9 copy-start.14
  138.8 1.1 copy-start.9
  139.9 1.5 copy-start.1
  139.9 1.5 copy-start.6
  147.8 1.0 copy-start.17
  147.8 1.1 copy-start.18
  147.8 1.1 copy-start.20
  147.9 209.8 %all-gather.2.cloned.1.call-start = ((), (), s32[]{:S(2)}) async-start(), calls=%async_computation.3 | async-start | bytes 8912896 | tf_op jit(solution)/shard_map/all_gather | solution.py:131
  149.0 2.0 copy-start.3
  150.9 1.1 copy-start.10
  152.0 1.2 copy-start.2
  153.2 3.9 %copy-start.22 = (f32[1,256]{1,0:T(1,128)S(1)}, f32[1,256]{1,0:T(1,128)}, u32[]{:S(2)}) copy-start(f32[1,256]{1,0:T(1,128)} %param.16) | copy-start | bytes 3076
  243.0 1.9 copy-start.15
  264.8 1.8 copy-start.4
  270.3 2.0 copy-start.19
  270.3 2.9 copy-start.7
Sparse Core Ops, SparseCore 0:
  22.3 93.0 all-reduce.2
  148.0 94.9 all-reduce.4
  273.3 84.2 all-gather.1
where the time goes:
time: 377 us; the launch traced here: 371 us
  waiting for transfers between devices  206 us (55%)
  matrix products  80.6 us (21%)
  blocking collectives  43.4 us (12%)
  other arithmetic  14 us (4%)
  between operations  14 us (4%)
  local copies, waits for them, and re-layouts  8.64 us (2%)
  starting transfers between devices  4.11 us (1%)
    psum x2, waiting for transfers between devices, body(): ortho = orthogonal(lax.psum(grads, 'ctx'))  165 us
    all_to_all x1, blocking collectives, body(): lax.all_to_all(out_proj, 'head', split_axis=1, concat_axis=0, tiled=True)  43.4 us
    all_gather x1, waiting for transfers between devices, body(): lax.all_gather(combined, 'head', axis=2, tiled=True)  40.8 us
    dot_general x18, matrix products, exact_dot(): jnp.dot(left, right, precision=highest, preferred_element_type=jnp.float32)  22.3 us
    dot_general x10, matrix products, orthogonal(): gram = jnp.einsum('mik,mjk->mij', iterate, iterate, precision=highest)  17 us
    dot_general x10, matrix products, quintic_step(): jnp.einsum('mij,mjk->mik', poly, iterate, precision=highest)  16.6 us
    dot_general x10, matrix products, quintic_step(): jnp.einsum('mij,mjk->mik', gram, gram, precision=highest)  9.34 us
  transfers between devices with their start and end apart: 4, of which 4 were waited for; matrix products, arithmetic and copies ran while one was open for 8% of the time, Pallas kernels for 0%

commit v1 on v0

--- a/solution.py
+++ b/solution.py
@@ -128,7 +128,9 @@
     proj_columns = lax.all_to_all(out_proj, "head", split_axis=1, concat_axis=0, tiled=True)
     summed = jnp.einsum(
         "ctf,fo->cto",
-        lax.all_gather(combined, "head", axis=2, tiled=True),
+        jnp.concatenate(
+            lax.all_to_all(jnp.stack([combined] * lax.axis_size("head")), "head", 0, 0), axis=2
+        ),
         proj_columns,
         preferred_element_type=jnp.float32,
     )

time: 377 us -> 415 us (1.10)
  blocking collectives: 43.4 us -> 104 us
  waiting for transfers between devices: 206 us -> 173 us
  local copies, waits for them, and re-layouts: 8.64 us -> 15.6 us
  starting transfers between devices: 4.11 us -> 10.5 us
    all_to_all x1, blocking collectives: 43.4 us -> 104 us  [body(): lax.all_to_all(jnp.stack([combined] * lax.axis_size('head')), 'head', 0, 0)]
    all_gather x1 -> x0, waiting for transfers between devices: 40.8 us -> none  [body(): lax.all_gather(combined, 'head', axis=2, tiled=True)]
    psum x2, waiting for transfers between devices: 165 us -> 173 us  [body(): ortho = orthogonal(lax.psum(grads, 'ctx'))]
    all_to_all x0 -> x1, starting transfers between devices: none -> 6.44 us  [body(): lax.all_to_all(out_proj, 'head', split_axis=1, concat_axis=0, tiled=True)]
  transfers between devices with their start and end apart: 4 -> 4, of which waited for: 4 -> 2; matrix products, arithmetic and copies ran while one was open for 8% -> 22% of each run, Pallas kernels for 0% -> 0%
where the time goes in v1:
time: 415 us; the launch traced here: 408 us
  waiting for transfers between devices  173 us (42%)
  blocking collectives  104 us (25%)
  matrix products  78.8 us (19%)
  local copies, waits for them, and re-layouts  15.6 us (4%)
  between operations  14.3 us (3%)
  other arithmetic  12.4 us (3%)
  starting transfers between devices  10.5 us (3%)
    psum x2, waiting for transfers between devices, body(): ortho = orthogonal(lax.psum(grads, 'ctx'))  173 us
    all_to_all x1, blocking collectives, body(): lax.all_to_all(jnp.stack([combined] * lax.axis_size('head')), 'head', 0, 0)  104 us
    dot_general x18, matrix products, exact_dot(): jnp.dot(left, right, precision=highest, preferred_element_type=jnp.float32)  22.2 us
    dot_general x10, matrix products, orthogonal(): gram = jnp.einsum('mik,mjk->mij', iterate, iterate, precision=highest)  17.7 us
    dot_general x10, matrix products, quintic_step(): jnp.einsum('mij,mjk->mik', poly, iterate, precision=highest)  16.2 us
    dot_general x10, matrix products, quintic_step(): jnp.einsum('mij,mjk->mik', gram, gram, precision=highest)  9.34 us
  transfers between devices with their start and end apart: 4, of which 2 were waited for; matrix products, arithmetic and copies ran while one was open for 22% of the time, Pallas kernels for 0%

profile of v1, /device:TPU:1, one launch (start us, length us, event | category | flops | bytes accessed | tf_op | source)
XLA Modules:
  0.0 408.1 jit_solution(11108295541599063590)
XLA Ops:
  6.5 1.3 fusion.32
  7.9 1.2 convert_divide_fusion
  9.2 1.0 fusion.75
  10.4 1.0 fusion.77
  11.6 1.1 fusion.66
  12.7 1.4 convolution_bitcast_fusion.3
  14.0 1.4 convolution_bitcast_fusion.5
  15.4 1.3 convolution_bitcast_fusion.4
  16.7 1.3 pad_maximum_fusion
  19.0 3.6 collective-permute-start
  22.6 3.3 copy.22
  25.8 2.4 copy.23
  28.2 6.4 %all-to-all-start.1 = ((bf16[256,16,256]{2,0,1:T(8,128)(2,1)}), bf16[256,16,256]{2,0,1:T(8,128)(2,1)}, u32[]{:S(2)}, u32[]{:S(2)}) async-start(bf16[256,16,256]{2,0,1:T(8,128)(2,1)} %copy.23), calls=%async_computation.1 | async-start | bytes 4194304 | tf_op jit(solution)/shard_map/all_to_all | solution.py:128
  36.4 1.0 copy.18
  38.1 1.2 convert_divide_fusion.1
  39.3 1.3 slice_select_fusion
  41.3 1.6 slice_bitcast_fusion.28
  42.9 2.1 fusion.141
  45.0 89.8 %all-reduce.3.cloned.1.call-done = f32[3,256,512]{2,1,0:T(8,128)} async-done(((f32[3,256,512]{2,1,0:T(8,128)}), f32[3,256,512]{2,1,0:T(8,128)}) %all-reduce.3.cloned.1.call-update) | async-done | bytes 1572880 | tf_op jit(solution)/shard_map/psum | solution.py:116
  134.8 1.8 multiply_reduce_fusion.1
  136.6 1.8 fusion.99
  139.4 1.8 multiply_add_fusion.9
  141.2 1.7 fusion.142
  142.9 0.9 fusion.25
  143.8 1.6 multiply_add_fusion.8
  145.4 1.8 fusion.143
  148.2 1.6 multiply_add_fusion.7
  149.8 1.7 fusion.144
  152.4 1.6 multiply_add_fusion.6
  154.0 1.7 fusion.145
  156.6 1.6 multiply_add_fusion.5
  158.2 1.0 fusion.71
  159.3 1.3 fusion.68
  160.6 1.1 fusion.80
  161.7 1.3 convolution_bitcast_fusion.1
  163.0 1.4 convolution_bitcast_fusion.2
  164.4 1.4 convolution_bitcast_fusion
  165.7 1.3 pad_maximum_fusion.1
  167.1 1.0 copy-done.20
  168.2 1.9 fusion.140
  170.1 1.0 fusion.73
  171.2 1.2 convolution_multiply_fusion.1
  172.4 1.9 multiply_reduce_fusion.3
  174.3 2.0 copy.19
  176.3 2.8 fusion.30
  179.1 83.1 %all-reduce.5.cloned.1.call-done = f32[3,256,512]{2,1,0:T(8,128)} async-done(((f32[3,256,512]{2,1,0:T(8,128)}), f32[3,256,512]{2,1,0:T(8,128)}) %all-reduce.5.cloned.1.call-update) | async-done | bytes 1572880 | tf_op jit(solution)/shard_map/psum | solution.py:116
  262.2 1.8 multiply_reduce_fusion
  264.1 2.3 fusion.100
  267.3 1.8 multiply_add_fusion.4
  269.1 1.7 fusion.146
  271.7 1.6 multiply_add_fusion.3
  273.3 1.7 fusion.147
  275.9 1.6 multiply_add_fusion.2
  277.5 1.8 fusion.148
  280.3 1.6 multiply_add_fusion.1
  281.9 1.7 fusion.149
  284.5 1.6 multiply_add_fusion
  286.1 1.1 fusion.60
  287.2 1.2 convolution_multiply_fusion
  288.4 1.2 multiply_reduce_fusion.2
  289.8 1.9 fusion.29
  291.8 0.9 stack.75
  292.7 103.6 %all_to_all.21 = bf16[16,2,512,256]{3,2,1,0:T(8,128)(2,1)S(1)} all-to-all(bf16[16,2,512,256]{3,2,1,0:T(8,128)(2,1)S(1)} %stack.75), channel_id=1, replica_groups=mesh['ctx'=8,'head'=16] {'head'}, dimensions={0} | all-to-all | bytes 16777216 | tf_op jit(solution)/shard_map/all_to_all | solution.py:132
  396.3 4.7 %fusion.12 = bf16[2,512,256]{2,1,0:T(8,128)(2,1)} fusion(bf16[256,16,256]{2,0,1:T(8,128)(2,1)} %all-to-all-done.1, bf16[16,2,512,256]{3,2,1,0:T(8,128)(2,1)S(1)} %all_to_all.21), kind=kOutput, calls=%fused_computation.33 | convolution fusion | flops 2147745792 | bytes 11010048 | tf_op jit(solution)/shard_map/ctf,fo->cto/dot_general | solution.py:129
  (85 shorter events, 13.4 us)
Async XLA Ops:
  6.5 2.6 copy-start
  6.5 128.2 %all-reduce.3.cloned.1.call-start = ((), (), s32[]{:S(2)}) async-start(), calls=%async_computation.2 | async-start | bytes 3145728 | tf_op jit(solution)/shard_map/psum | solution.py:116
  9.1 8.9 %copy-start.6 = (bf16[2,512,256]{2,1,0:T(8,128)(2,1)}, bf16[2,512,256]{2,1,0:T(8,128)(2,1)S(1)}, u32[]{:S(2)}) copy-start(bf16[2,512,256]{2,1,0:T(8,128)(2,1)S(1)} %get-tuple-element.8) | copy-start | bytes 1572868
  9.1 1.2 copy-start.11
  10.4 1.0 copy-start.25
  10.4 1.1 copy-start.8
  10.4 1.2 copy-start.14
  19.0 20.3 %collective-permute-start = (bf16[2,2,256,256]{3,2,1,0:T(8,128)(2,1)}, bf16[2,2,256,256]{3,2,1,0:T(8,128)(2,1)}, u32[]{:S(2)}, u32[]{:S(2)}) collective-permute-start(bf16[2,2,256,256]{3,2,1,0:T(8,128)(2,1)} %pad_maximum_fusion.2), channel_id=1, source_target_pairs={{0,16},{16,32},{32,48},{48,64},{64,80},{80,96},{96,112},{112,0},{1... | collective-permute-start | bytes 1572872 | tf_op jit(solution)/shard_map/ppermute | solution.py:19
  28.2 7.0 %copy-start.7 = (bf16[2,512,256]{2,1,0:T(8,128)(2,1)S(1)}, bf16[2,512,256]{2,1,0:T(8,128)(2,1)}, u32[]{:S(2)}) copy-start(bf16[2,512,256]{2,1,0:T(8,128)(2,1)} %copy-done.6) | copy-start | bytes 1572868
  28.2 7.9 %copy-start.16 = (bf16[2,512,256]{2,1,0:T(8,128)(2,1)S(1)}, bf16[2,512,256]{2,1,0:T(8,128)(2,1)}, u32[]{:S(2)}) copy-start(bf16[2,512,256]{2,1,0:T(8,128)(2,1)} %param.9) | copy-start | bytes 1572868
  28.2 263.5 %all-to-all-start.1 = ((bf16[256,16,256]{2,0,1:T(8,128)(2,1)}), bf16[256,16,256]{2,0,1:T(8,128)(2,1)}, u32[]{:S(2)}, u32[]{:S(2)}) async-start(bf16[256,16,256]{2,0,1:T(8,128)(2,1)} %copy.23), calls=%async_computation.1 | async-start | bytes 4194304 | tf_op jit(solution)/shard_map/all_to_all | solution.py:128
  34.7 1.7 copy-start.15
  34.7 2.7 copy-start.9
  34.7 227.5 %all-reduce.5.cloned.1.call-start = ((), (), s32[]{:S(2)}) async-start(), calls=%async_computation.3 | async-start | bytes 3145728 | tf_op jit(solution)/shard_map/psum | solution.py:116
  38.1 4.8 %copy-start.23 = (bf16[512,256]{1,0:T(8,128)(2,1)S(1)}, bf16[512,256]{1,0:T(8,128)(2,1)}, u32[]{:S(2)}) copy-start(bf16[512,256]{1,0:T(8,128)(2,1)} %get-tuple-element.13) | copy-start | bytes 786436
  39.3 3.6 copy-start.19
  134.8 1.9 copy-start.17
  156.6 1.6 copy-start.1
  158.2 1.1 copy-start.12
  159.2 1.3 copy-start.2
  159.3 1.3 copy-start.10
  167.0 1.0 copy-start.20
  167.0 1.1 copy-start.21
  167.0 1.1 copy-start.24
  168.2 1.9 copy-start.4
  170.1 1.1 copy-start.13
  171.2 1.2 copy-start.3
  172.4 4.0 copy-start.26
  262.2 1.9 copy-start.18
  284.5 1.6 copy-start.5
  289.8 1.9 copy-start.22
Sparse Core Ops, SparseCore 0:
  18.2 116.5 all-reduce.2
  167.2 94.9 all-reduce.4
